TPU v7x, 32 devices: a whole 2x2x4 slice. The times are simulated.
32 devices in a mesh: space: 4 (over y, x), tm: 8 (over z, core).
Axes of the slice: x: 2, y: 2, z: 4, core: 2. Of those that a mesh axis runs over, the one named last changes fastest.
Arguments:
- snapshots: float32 [4096, 4096], P('space', 'tm'), may hold values from -6 to 6
- test_seeds: int32 [2], replicated, may hold values from 0 to 16777215
- block_offsets: int32 [2], replicated, may hold values from 0 to 4095
Outputs:
- residual: float32 [4096, 4096], P('space', 'tm')
- factor: float32 [512, 512], replicated
Inputs may be any that keep to these rules, and one draw needn't show every extreme that they name: `test_seeds`: seeds of the two test matrices.
All inputs are finite; a program needn't handle non-finite values.
Results may differ from a plain program's by a relative error of at most 0.0003.
Values sent between devices are 32-bit elements; how exact they have to be, the bound alone decides.
A program may use at most 128 MiB of HBM per device.

v0:
```python
import math

import jax
import jax.numpy as jnp
from jax import lax
from jax.sharding import PartitionSpec as P

RANGE = 512
CORANGE = 1024


PRECISE = lax.Precision.HIGHEST


def scramble(values):
    values = jnp.bitwise_xor(values, lax.shift_right_logical(values, jnp.int32(16)))
    values = values * 73244475
    values = jnp.bitwise_xor(values, lax.shift_right_logical(values, jnp.int32(16)))
    values = values * 73244475
    values = jnp.bitwise_xor(values, lax.shift_right_logical(values, jnp.int32(16)))
    return values


def gaussian_table(row_ids, col_ids, seed_value):
    row_hash = scramble(row_ids * 668265261 + seed_value)
    cell_hash = scramble(jnp.bitwise_xor(row_hash[:, None], col_ids[None, :] * 374761393))
    running = jnp.zeros(cell_hash.shape, jnp.float32)
    for stream in range(4):
        hashed = scramble(cell_hash + stream * 625341585)
        running = running + jnp.bitwise_and(hashed, 16777215).astype(jnp.float32) * (
            1.0 / 16777216.0
        )
    return (running - 2.0) * math.sqrt(3.0)


def gram_dot(left_side, right_side):
    return lax.dot_general(left_side, right_side, (((0,), (0,)), ((), ())), precision=PRECISE)


def tri_apply(lower_factor, sketch_part):
    return jax.scipy.linalg.solve_triangular(lower_factor, sketch_part.T, lower=True).T


def local(snapshots, test_seeds, block_offsets):
    space_index = lax.axis_index("space")
    time_index = lax.axis_index("tm")
    cell_rows = snapshots.shape[0]
    snap_cols = snapshots.shape[1]
    cells_total = cell_rows * lax.axis_size("space")
    snaps_total = snap_cols * lax.axis_size("tm")
    cell_ids = (
        block_offsets[0] * cells_total
        + space_index * cell_rows
        + jnp.arange(cell_rows, dtype=jnp.int32)
    )
    snap_ids = (
        block_offsets[1] * snaps_total
        + time_index * snap_cols
        + jnp.arange(snap_cols, dtype=jnp.int32)
    )
    omega_test = gaussian_table(
        snap_ids, jnp.arange(RANGE, dtype=jnp.int32), test_seeds[0]
    ) / math.sqrt(cells_total * snaps_total)
    psi_test = gaussian_table(
        cell_ids, jnp.arange(CORANGE, dtype=jnp.int32), test_seeds[1]
    ) / math.sqrt(cells_total)
    partial_range = jnp.dot(snapshots, omega_test, precision=PRECISE)
    range_sketch = lax.psum(partial_range, "tm")
    first_gram = lax.psum(gram_dot(range_sketch, range_sketch), "space")
    first_factor = jnp.linalg.cholesky(first_gram)
    range_basis = tri_apply(first_factor, range_sketch)
    factor = first_factor.T
    coupling = lax.psum(gram_dot(psi_test, range_basis), "space")
    normal = gram_dot(coupling, coupling)
    core_factor = jnp.linalg.cholesky(normal)
    lifted = jnp.dot(psi_test, coupling, precision=PRECISE)
    projected = lax.psum(gram_dot(lifted, snapshots), "space")
    core_matrix = jax.scipy.linalg.cho_solve((core_factor, True), projected)
    residual = snapshots - jnp.dot(range_basis, core_matrix, precision=PRECISE)
    return (residual, factor)


def solution(mesh):
    return jax.shard_map(
        local,
        mesh=mesh,
        in_specs=(P("space", "tm"), P(), P()),
        out_specs=(P("space", "tm"), P()),
        check_vma=False,
    )
```

profile of v0, /device:TPU:0, one launch (start us, length us, event | category | flops | bytes accessed | tf_op | source)
XLA Modules:
  0.0 573.4 jit_solution(16064575732171119809)
XLA Ops:
  7.2 1.3 fusion.197
  8.5 1.3 fusion.196
  11.2 11.5 %convolution_bitcast_fusion = f32[1024,512]{0,1:T(8,128)} fusion(f32[1024,512]{1,0:T(8,128)} %param.4, s32[512]{0:T(512)S(1)} %get-tuple-element.72, s32[512]{0:T(512)S(1)} %get-tuple-element.71), kind=kOutput, calls=%fused_computation.46 | convolution fusion | flops 3236429824 | bytes 4198400 | tf_op jit(solution)/shard_map/dot_general | solution.py:67
  23.3 67.2 %all-reduce.6.cloned.1.call-done = f32[1024,512]{0,1:T(8,128)} async-done(((f32[1024,512]{0,1:T(8,128)}), f32[1024,512]{0,1:T(8,128)}) %all-reduce.6.cloned.1.call-update) | async-done | bytes 2097168 | tf_op jit(solution)/shard_map/psum | solution.py:68
  90.5 6.7 %fusion.198 = f32[512,512]{0,1:T(8,128)} fusion(f32[1024,512]{0,1:T(8,128)} %all-reduce.6.cloned.1.call-done), kind=kOutput, calls=%fused_computation.299 | convolution fusion | flops 3221225472 | bytes 3145728 | tf_op jit(solution)/shard_map/dot_general | solution.py:37
  98.6 51.0 %all-reduce.8.cloned.1.call-done = f32[512,512]{0,1:T(8,128)} async-done(((f32[512,512]{0,1:T(8,128)}), f32[512,512]{0,1:T(8,128)}) %all-reduce.8.cloned.1.call-update) | async-done | bytes 1048592 | tf_op jit(solution)/shard_map/psum | solution.py:69
  149.5 1.6 copy.6
  151.4 11.7 %cholesky.286 = f32[128,128]{1,0:T(8,128)S(1)} custom-call(f32[128,128]{1,0:T(8,128)S(1)} %cholesky.426), custom_call_target="Cholesky" | custom-call | tf_op jit(solution)/shard_map/jit(cholesky)/cholesky | solution.py:70
  163.3 9.8 %custom-call.36 = f32[1,128,128]{1,2,0:T(8,128)S(1)} custom-call(f32[1,128,128]{2,1,0:T(8,128)S(1)} %get-tuple-element.62), custom_call_target="InvertDiagBlocksLowerTriangular" | custom-call | tf_op jit(solution)/shard_map/jit(cholesky)/cholesky | solution.py:70
  173.8 11.7 %cholesky.305 = f32[128,128]{1,0:T(8,128)S(1)} custom-call(f32[128,128]{1,0:T(8,128)S(1)} %cholesky.430), custom_call_target="Cholesky" | custom-call | tf_op jit(solution)/shard_map/jit(cholesky)/cholesky | solution.py:70
  185.5 10.0 %custom-call.37 = f32[1,128,128]{1,2,0:T(8,128)S(1)} custom-call(f32[1,128,128]{2,1,0:T(8,128)S(1)} %get-tuple-element.59), custom_call_target="InvertDiagBlocksLowerTriangular" | custom-call | tf_op jit(solution)/shard_map/jit(cholesky)/cholesky | solution.py:70
  196.2 11.7 %cholesky.326 = f32[128,128]{1,0:T(8,128)S(1)} custom-call(f32[128,128]{1,0:T(8,128)S(1)} %cholesky.435), custom_call_target="Cholesky" | custom-call | tf_op jit(solution)/shard_map/jit(cholesky)/cholesky | solution.py:70
  207.9 9.8 %custom-call.38 = f32[1,128,128]{1,2,0:T(8,128)S(1)} custom-call(f32[1,128,128]{2,1,0:T(8,128)S(1)} %get-tuple-element.56), custom_call_target="InvertDiagBlocksLowerTriangular" | custom-call | tf_op jit(solution)/shard_map/jit(cholesky)/cholesky | solution.py:70
  218.3 11.7 %cholesky.343 = f32[128,128]{1,0:T(8,128)S(1)} custom-call(f32[128,128]{1,0:T(8,128)S(1)} %convolution_subtract_fusion.14), custom_call_target="Cholesky" | custom-call | tf_op jit(solution)/shard_map/jit(cholesky)/cholesky | solution.py:70
  235.3 2.0 fusion.82
  237.3 11.9 %while.2 = (s32[]{:T(128)}, f32[512,512]{1,0:T(8,128)}, s32[4,2]{0,1:T(2,128)S(1)}, f32[4,128,128]{2,1,0:T(8,128)S(1)}, s32[]{:T(128)}) while((s32[]{:T(128)}, f32[512,512]{1,0:T(8,128)}, s32[4,2]{0,1:T(2,128)S(1)}, f32[4,128,128]{2,1,0:T(8,128)S(1)}, s32[]{:T(128)}) %tuple.58), condition=%wide.while_cond, body=%wide.while_body.sunk | while | flops 2 | bytes 131189 | solution.py:41
  238.0 2.3 bitcast_dynamic-update-slice_fusion.4
  241.0 2.3 bitcast_dynamic-update-slice_fusion.4
  244.0 2.3 bitcast_dynamic-update-slice_fusion.4
  247.0 2.2 bitcast_dynamic-update-slice_fusion.4
  249.3 39.3 %custom-call.31 = f32[4,128,128]{1,2,0:T(8,128)S(1)} custom-call(f32[4,128,128]{2,1,0:T(8,128)S(1)} %get-tuple-element.10), custom_call_target="InvertDiagBlocksLowerTriangular" | custom-call | tf_op jit(solution)/shard_map/jit(_solve_triangular)/triangular_solve | solution.py:41
  289.3 1.4 convolution_subtract_fusion.2
  291.3 1.6 convolution_subtract_fusion.1
  293.6 2.2 fusion.34
  297.3 22.5 %fusion.26 = f32[1024,512]{1,0:T(8,128)} fusion(s32[1024]{0:T(1024)S(1)} %get-tuple-element.74, s32[1024]{0:T(1024)S(1)} %get-tuple-element.73, f32[128,1024]{1,0:T(8,128)S(1)} %fusion.136, f32[128,1024]{1,0:T(8,128)S(1)} %fusion.137, f32[128,1024]{1,0:T(8,128)S(1)} %fusion.139, f32[128,1024]{1,0:T(8,128)S(1)} %fusion.93), kind=kOutput, calls=%fused_computation.45 | convolution fusion | flops 6504841216 | bytes 4202496 | tf_op jit(solution)/shard_map/dot_general | solution.py:37
  321.0 1.3 copy.8
  322.3 67.3 %all-reduce.10.cloned.1.call-done = f32[1024,512]{1,0:T(8,128)} async-done(((f32[1024,512]{1,0:T(8,128)}), f32[1024,512]{1,0:T(8,128)}) %all-reduce.10.cloned.1.call-update) | async-done | bytes 2097168 | tf_op jit(solution)/shard_map/psum | solution.py:73
  389.6 16.2 %fusion.24 = f32[1024,512]{1,0:T(8,128)S(1)} fusion(f32[1024,512]{1,0:T(8,128)} %all-reduce.10.cloned.1.call-done, s32[1024]{0:T(1024)S(1)} %get-tuple-element.74, s32[1024]{0:T(1024)S(1)} %get-tuple-element.73), kind=kOutput, calls=%fused_computation.44 | convolution fusion | flops 6503268352 | bytes 4202496 | tf_op jit(solution)/shard_map/dot_general | solution.py:76
  405.9 4.6 fusion.200
  410.5 5.7 fusion.199
  417.8 11.9 %cholesky.358 = f32[128,128]{1,0:T(8,128)S(1)} custom-call(f32[128,128]{1,0:T(8,128)S(1)} %cholesky.439), custom_call_target="Cholesky" | custom-call | tf_op jit(solution)/shard_map/jit(cholesky)/cholesky | solution.py:75
  429.8 9.8 %custom-call.39 = f32[1,128,128]{1,2,0:T(8,128)S(1)} custom-call(f32[1,128,128]{2,1,0:T(8,128)S(1)} %get-tuple-element.52), custom_call_target="InvertDiagBlocksLowerTriangular" | custom-call | tf_op jit(solution)/shard_map/jit(cholesky)/cholesky | solution.py:75
  440.9 1.3 convolution_subtract_fusion.9
  442.2 11.7 %cholesky.377 = f32[128,128]{1,0:T(8,128)S(1)} custom-call(f32[128,128]{1,0:T(8,128)S(1)} %cholesky.443), custom_call_target="Cholesky" | custom-call | tf_op jit(solution)/shard_map/jit(cholesky)/cholesky | solution.py:75
  453.9 9.8 %custom-call.40 = f32[1,128,128]{1,2,0:T(8,128)S(1)} custom-call(f32[1,128,128]{2,1,0:T(8,128)S(1)} %get-tuple-element.49), custom_call_target="InvertDiagBlocksLowerTriangular" | custom-call | tf_op jit(solution)/shard_map/jit(cholesky)/cholesky | solution.py:75
  464.0 1.3 convolution_subtract_fusion.11
  465.3 12.1 %cholesky.398 = f32[128,128]{1,0:T(8,128)S(1)} custom-call(f32[128,128]{1,0:T(8,128)S(1)} %cholesky.448), custom_call_target="Cholesky" | custom-call | tf_op jit(solution)/shard_map/jit(cholesky)/cholesky | solution.py:75
  477.4 9.8 %custom-call.41 = f32[1,128,128]{1,2,0:T(8,128)S(1)} custom-call(f32[1,128,128]{2,1,0:T(8,128)S(1)} %get-tuple-element.46), custom_call_target="InvertDiagBlocksLowerTriangular" | custom-call | tf_op jit(solution)/shard_map/jit(cholesky)/cholesky | solution.py:75
  488.7 11.7 %cholesky.415 = f32[128,128]{1,0:T(8,128)S(1)} custom-call(f32[128,128]{1,0:T(8,128)S(1)} %convolution_subtract_fusion.13), custom_call_target="Cholesky" | custom-call | tf_op jit(solution)/shard_map/jit(cholesky)/cholesky | solution.py:75
  505.8 8.3 %while.3 = (s32[]{:T(128)}, f32[512,512]{1,0:T(8,128)S(1)}, s32[4,2]{0,1:T(2,128)S(1)}, f32[4,128,128]{2,1,0:T(8,128)S(1)}, s32[]{:T(128)}) while((s32[]{:T(128)}, f32[512,512]{1,0:T(8,128)S(1)}, s32[4,2]{0,1:T(2,128)S(1)}, f32[4,128,128]{2,1,0:T(8,128)S(1)}, s32[]{:T(128)}) %tuple.72), condition=%wide.while_cond.1, body=%wide.while_body.1.sunk | while | flops 2 | bytes 131189 | solution.py:78
  506.7 1.3 bitcast_dynamic-update-slice_fusion.5
  508.7 1.3 bitcast_dynamic-update-slice_fusion.5
  510.8 1.3 bitcast_dynamic-update-slice_fusion.5
  512.8 1.3 bitcast_dynamic-update-slice_fusion.5
  514.2 39.3 %custom-call.32 = f32[4,128,128]{1,2,0:T(8,128)S(1)} custom-call(f32[4,128,128]{2,1,0:T(8,128)S(1)} %get-tuple-element.18), custom_call_target="InvertDiagBlocksLowerTriangular" | custom-call | tf_op jit(solution)/shard_map/jit(_cho_solve)/triangular_solve | solution.py:78
  553.5 1.5 fusion.112
  555.0 1.3 convolution_subtract_fusion.6
  561.8 4.9 convolution_subtract_fusion
  (107 shorter events, 29.9 us)
Async XLA Ops:
  7.2 83.3 %all-reduce.6.cloned.1.call-start = ((), (), s32[]{:S(2)}) async-start(), calls=%async_computation | async-start | bytes 4194304 | tf_op jit(solution)/shard_map/psum | solution.py:68
  22.7 126.8 %all-reduce.8.cloned.1.call-start = ((), (), s32[]{:S(2)}) async-start(), calls=%async_computation.1 | async-start | bytes 2097152 | tf_op jit(solution)/shard_map/psum | solution.py:69
  97.2 292.5 %all-reduce.10.cloned.1.call-start = ((), (), s32[]{:S(2)}) async-start(), calls=%async_computation.2 | async-start | bytes 4194304 | tf_op jit(solution)/shard_map/psum | solution.py:73
  149.5 1.7 copy-start.5
  235.3 53.3 %copy-start = (f32[1024,512]{0,1:T(8,128)S(1)}, f32[1024,512]{0,1:T(8,128)}, u32[]{:S(2)}) copy-start(f32[1024,512]{0,1:T(8,128)} %all-reduce.6.cloned.1.call-done) | copy-start | bytes 6291460
  293.6 2.9 copy-start.3
  296.5 0.8 copy-start.8
  319.8 1.2 copy-start.6
  319.8 233.7 %all-reduce.12.cloned.1.call-start = ((), (), s32[]{:S(2)}) async-start(), calls=%async_computation.3 | async-start | bytes 2097152 | tf_op jit(solution)/shard_map/psum | solution.py:77
  322.3 83.5 %copy-start.1 = (f32[1024,512]{1,0:T(8,128)S(1)}, f32[1024,512]{1,0:T(8,128)}, u32[]{:S(2)}) copy-start(f32[1024,512]{1,0:T(8,128)} %param.4) | copy-start | bytes 6291460
  416.8 1.0 copy-start.7
  553.5 3.2 copy-start.10
  559.5 2.3 copy-start.2
  559.5 2.3 copy-start.4
  559.5 2.3 copy-start.9
Sparse Core Ops, SparseCore 0:
  22.9 67.5 all-reduce.5
  97.3 52.1 all-reduce.7
  319.9 69.6 all-reduce.9
  410.6 52.9 all-reduce.11
where the time goes:
time: 581 us; the launch traced here: 573 us
  other arithmetic  241 us (41%)
  waiting for transfers between devices  186 us (32%)
  matrix products  95.4 us (16%)
  local copies, waits for them, and re-layouts  29.1 us (5%)
  between operations  21 us (4%)
    another operation x15, other arithmetic, local(): core_factor = jnp.linalg.cholesky(normal)  79.7 us
    another operation x15, other arithmetic, local(): first_factor = jnp.linalg.cholesky(first_gram)  79.2 us
    psum x1, waiting for transfers between devices, local(): coupling = lax.psum(gram_dot(psi_test, range_basis), 'space')  67.3 us
    psum x1, waiting for transfers between devices, local(): range_sketch = lax.psum(partial_range, 'tm')  67.2 us
    psum x1, waiting for transfers between devices, local(): first_gram = lax.psum(gram_dot(range_sketch, range_sketch), 'space')  51 us
    dot_general x4, matrix products, gram_dot(): lax.dot_general(left_side, right_side, (((0,), (0,)), ((), ())), precisio...  39.5 us
    another operation x2, other arithmetic, local(): core_matrix = jax.scipy.linalg.cho_solve((core_factor, True), projected)  39.4 us
    another operation x2, other arithmetic, tri_apply(): jax.scipy.linalg.solve_triangular(lower_factor, sketch_part.T, lower=True)  39.3 us
  transfers between devices with their start and end apart: 4, of which 3 were waited for; matrix products, arithmetic and copies ran while one was open for 25% of the time, Pallas kernels for 0%

commit v1 on v0

--- a/solution.py
+++ b/solution.py
@@ -3,11 +3,13 @@
 import jax
 import jax.numpy as jnp
 from jax import lax
+from jax.experimental import pallas as pl
+from jax.experimental.pallas import tpu as pltpu
 from jax.sharding import PartitionSpec as P
 
 RANGE = 512
 CORANGE = 1024
-
+BLOCK = 32
 
 PRECISE = lax.Precision.HIGHEST
 
@@ -34,11 +36,88 @@
 
 
 def gram_dot(left_side, right_side):
-    return lax.dot_general(left_side, right_side, (((0,), (0,)), ((), ())), precision=PRECISE)
+    return lax.dot_general(
+        left_side, right_side, (((0,), (0,)), ((), ())), precision=PRECISE,
+        preferred_element_type=jnp.float32,
+    )
 
 
-def tri_apply(lower_factor, sketch_part):
-    return jax.scipy.linalg.solve_triangular(lower_factor, sketch_part.T, lower=True).T
+def dot(left_side, right_side):
+    return jnp.dot(
+        left_side, right_side, precision=PRECISE, preferred_element_type=jnp.float32
+    )
+
+
+def eliminate(blocks):
+    size = blocks[0].shape[0]
+    row_id = lax.broadcasted_iota(jnp.int32, (size, size), 0)
+    col_id = lax.broadcasted_iota(jnp.int32, (size, size), 1)
+    eye = jnp.where(row_id == col_id, 1.0, 0.0).astype(jnp.float32)
+    work = [(block, eye) for block in blocks]
+    for step in range(size - 1):
+        later = []
+        for block, inverse in work:
+            pivot_row = block[step : step + 1, :]
+            scaled = pivot_row / block[step : step + 1, step : step + 1]
+            inv_row = inverse[step : step + 1, :] / block[step : step + 1, step : step + 1]
+            column = jnp.where(row_id > step, block[:, step : step + 1], 0.0)
+            later.append((block - column * scaled, inverse - column * inv_row))
+        work = later
+    factors = []
+    for block, inverse in work:
+        diagonal = jnp.sum(jnp.where(row_id == col_id, block, 0.0), axis=1, keepdims=True)
+        factors.append(inverse / jnp.sqrt(diagonal))
+    return factors
+
+
+def factor_kernel(gram_ref, normal_ref, rhs_ref, factor_ref, out_ref, g, s, inv):
+    n = gram_ref.shape[0]
+    width = rhs_ref.shape[1]
+    g[...] = gram_ref[...]
+    s[:, :n] = normal_ref[...]
+    s[:, n:] = rhs_ref[...]
+    factor_ref[...] = jnp.zeros_like(factor_ref)
+    for lo in range(0, n, BLOCK):
+        hi = lo + BLOCK
+        base = lo // 128 * 128
+        first, second = eliminate([g[lo:hi, lo:hi], s[lo:hi, lo:hi]])
+        inv[lo:hi, :] = second
+        g_panel = dot(first, g[lo:hi, base:])
+        s_panel = dot(second, s[lo:hi, base:])
+        s[lo:hi, base:] = s_panel
+        rows = lax.broadcasted_iota(jnp.int32, g_panel.shape, 0) + lo
+        cols = lax.broadcasted_iota(jnp.int32, g_panel.shape, 1) + base
+        factor_ref[lo:hi, base:] = jnp.where(cols >= rows, g_panel, 0.0)
+        if hi < n:
+            after = hi // 128 * 128
+            g[hi:, after:] -= gram_dot(g_panel[:, hi - base :], g_panel[:, after - base :])
+            s[hi:, after:] -= gram_dot(s_panel[:, hi - base : n - base], s_panel[:, after - base :])
+    for lo in range(n - BLOCK, -1, -BLOCK):
+        hi = lo + BLOCK
+        part = s[lo:hi, n:]
+        if hi < n:
+            part = part - dot(s[lo:hi, hi:n], out_ref[hi:, :])
+        out_ref[lo:hi, :] = gram_dot(inv[lo:hi, :], part)
+
+
+def factor_and_solve(gram, normal, rhs):
+    n, width = rhs.shape
+    return pl.pallas_call(
+        factor_kernel,
+        out_shape=(
+            jax.ShapeDtypeStruct((n, n), jnp.float32),
+            jax.ShapeDtypeStruct((n, width), jnp.float32),
+        ),
+        in_specs=[pl.BlockSpec(memory_space=pltpu.VMEM)] * 3,
+        out_specs=(pl.BlockSpec(memory_space=pltpu.VMEM),) * 2,
+        scratch_shapes=[
+            pltpu.VMEM((n, n), jnp.float32),
+            pltpu.VMEM((n, n + width), jnp.float32),
+            pltpu.VMEM((n, BLOCK), jnp.float32),
+        ],
+        compiler_params=pltpu.CompilerParams(vmem_limit_bytes=40 * 1024 * 1024),
+        name="factor_and_solve",
+    )(gram, normal, rhs)
 
 
 def local(snapshots, test_seeds, block_offsets):
@@ -64,19 +143,17 @@
     psi_test = gaussian_table(
         cell_ids, jnp.arange(CORANGE, dtype=jnp.int32), test_seeds[1]
     ) / math.sqrt(cells_total)
+    psi_test = lax.optimization_barrier(psi_test)
     partial_range = jnp.dot(snapshots, omega_test, precision=PRECISE)
     range_sketch = lax.psum(partial_range, "tm")
-    first_gram = lax.psum(gram_dot(range_sketch, range_sketch), "space")
-    first_factor = jnp.linalg.cholesky(first_gram)
-    range_basis = tri_apply(first_factor, range_sketch)
-    factor = first_factor.T
-    coupling = lax.psum(gram_dot(psi_test, range_basis), "space")
-    normal = gram_dot(coupling, coupling)
-    core_factor = jnp.linalg.cholesky(normal)
-    lifted = jnp.dot(psi_test, coupling, precision=PRECISE)
-    projected = lax.psum(gram_dot(lifted, snapshots), "space")
-    core_matrix = jax.scipy.linalg.cho_solve((core_factor, True), projected)
-    residual = snapshots - jnp.dot(range_basis, core_matrix, precision=PRECISE)
+    corange_sketch = lax.psum(gram_dot(psi_test, snapshots), "space")
+    range_sketch, corange_sketch = lax.optimization_barrier((range_sketch, corange_sketch))
+    mixed = lax.psum(gram_dot(psi_test, range_sketch), "space")
+    gram = lax.psum(gram_dot(range_sketch, range_sketch), "space")
+    normal = gram_dot(mixed, mixed)
+    rhs = gram_dot(mixed, corange_sketch)
+    factor, weights = factor_and_solve(gram, normal, rhs)
+    residual = snapshots - jnp.dot(range_sketch, weights, precision=PRECISE)
     return (residual, factor)
 
 

time: 581 us -> 367 us (0.63)
  other arithmetic: 241 us -> 9.35 us
  Pallas kernels: 0 us -> 67.4 us
  matrix products: 95.4 us -> 55.6 us
  local copies, waits for them, and re-layouts: 29.1 us -> 4.66 us
  waiting for transfers between devices: 186 us -> 208 us
    another operation x34 -> x0, other arithmetic: 238 us -> none  [the longest x15 79.7 us: local(): core_factor = jnp.linalg.cholesky(normal)]
    pallas_call x0 -> x1, Pallas kernels: none -> 67.4 us  [factor_and_solve(): pl.pallas_call(factor_kernel, out_shape=(jax.ShapeDtypeStruct((n, n), jnp...]
    psum x3 -> x2, waiting for transfers between devices: 118 us -> 160 us  [the longest x1 87.5 us: local(): gram = lax.psum(gram_dot(range_sketch, range_sketch), 'space')]
    another operation x33 -> x0, matrix products: 23.2 us -> none  [the longest x14 8.12 us: local(): core_matrix = jax.scipy.linalg.cho_solve((core_factor, True), projected)]
    another operation x33 -> x0, local copies, waits for them, and re-layouts: 20.2 us -> none
    psum x1, waiting for transfers between devices: 67.2 us -> 47.6 us  [local(): range_sketch = lax.psum(partial_range, 'tm')]
    dot_general x2 -> x1, matrix products: 21.1 us -> 4.8 us  [local(): residual = snapshots - jnp.dot(range_sketch, weights, precision=PRECISE)]
    div x2 -> x1, other arithmetic: 0.45 us -> 8.03 us  [local(): gaussian_table(cell_ids, jnp.arange(CORANGE, dtype=jnp.int32), test_seeds...]
  transfers between devices with their start and end apart: 4 -> 3, of which waited for: 3 -> 3; matrix products, arithmetic and copies ran while one was open for 25% -> 5% of each run, Pallas kernels for 0% -> 0%
where the time goes in v1:
time: 367 us; the launch traced here: 361 us
  waiting for transfers between devices  208 us (57%)
  Pallas kernels  67.4 us (18%)
  matrix products  55.6 us (15%)
  between operations  15.7 us (4%)
  other arithmetic  9.35 us (3%)
  local copies, waits for them, and re-layouts  4.66 us (1%)
    psum x1, waiting for transfers between devices, local(): gram = lax.psum(gram_dot(range_sketch, range_sketch), 'space')  87.5 us
    psum x1, waiting for transfers between devices, local(): corange_sketch = lax.psum(gram_dot(psi_test, snapshots), 'space')  72.4 us
    pallas_call x1, Pallas kernels, factor_and_solve(): pl.pallas_call(factor_kernel, out_shape=(jax.ShapeDtypeStruct((n, n), jnp...  67.4 us
    psum x1, waiting for transfers between devices, local(): range_sketch = lax.psum(partial_range, 'tm')  47.6 us
    dot_general x5, matrix products, gram_dot(): lax.dot_general(left_side, right_side, (((0,), (0,)), ((), ())), precisio...  39.3 us
    dot_general x1, matrix products, local(): partial_range = jnp.dot(snapshots, omega_test, precision=PRECISE)  11.5 us
    div x1, other arithmetic, local(): gaussian_table(cell_ids, jnp.arange(CORANGE, dtype=jnp.int32), test_seeds...  8.03 us
  transfers between devices with their start and end apart: 3, of which 3 were waited for; matrix products, arithmetic and copies ran while one was open for 5% of the time, Pallas kernels for 0%

profile of v1, /device:TPU:0, one launch (start us, length us, event | category | flops | bytes accessed | tf_op | source)
XLA Modules:
  0.0 360.6 jit_solution(14663687532242262919)
XLA Ops:
  7.2 0.0 all-reduce.5.cloned.1.call-start
  7.2 1.3 fusion.81
  8.5 1.4 fusion.80
  10.5 0.7 shift-right-logical_xor_fusion.34
  11.2 11.5 %convolution_bitcast_fusion = f32[1024,512]{0,1:T(8,128)} fusion(f32[1024,512]{1,0:T(8,128)} %param.3, s32[512]{0:T(512)S(1)} %get-tuple-element.17, s32[512]{0:T(512)S(1)} %get-tuple-element.16), kind=kOutput, calls=%fused_computation.39 | convolution fusion | flops 3236429824 | bytes 4198400 | tf_op jit(solution)/shard_map/dot_general | solution.py:147
  22.7 0.0 copy-start.4
  22.7 0.0 all-reduce.5.cloned.1.call-update
  22.8 0.2 all-reduce.7.cloned.1.call-start
  23.7 0.7 shift-right-logical_xor_fusion.31
  24.4 8.0 %fusion.11 = f32[1024,1024]{1,0:T(8,128)S(1)} fusion(s32[1024]{0:T(1024)S(1)} %get-tuple-element.19, s32[1024]{0:T(1024)S(1)} %get-tuple-element.18), kind=kLoop, calls=%fused_computation.26 | loop fusion | flops 60817408 | bytes 4202496 | tf_op jit(solution)/shard_map/div | solution.py:143
  32.4 0.0 copy-start.1
  32.4 1.9 copy-done.1
  34.4 0.0 copy-done.4
  34.4 8.4 %fusion.82 = f32[1024,512]{1,0:T(8,128)} fusion(f32[1024,1024]{1,0:T(8,128)S(1)} %fusion.11, f32[1024,512]{1,0:T(8,128)S(1)} %copy-done.4), kind=kOutput, calls=%fused_computation.118 | convolution fusion | flops 6442450944 | bytes 8388608 | tf_op jit(solution)/shard_map/dot_general | solution.py:39
  42.8 0.0 all-reduce.7.cloned.1.call-update
  42.8 0.0 all-reduce.9.cloned.1.call-start
  42.9 47.6 %all-reduce.5.cloned.1.call-done = f32[1024,512]{0,1:T(8,128)} async-done(((f32[1024,512]{0,1:T(8,128)}), f32[1024,512]{0,1:T(8,128)}) %all-reduce.5.cloned.1.call-update) | async-done | bytes 2097168 | tf_op jit(solution)/shard_map/psum | solution.py:148
  90.5 0.0 copy-start.2
  90.5 72.4 %all-reduce.7.cloned.1.call-done = f32[1024,512]{1,0:T(8,128)} async-done(((f32[1024,512]{1,0:T(8,128)}), f32[1024,512]{1,0:T(8,128)}) %all-reduce.7.cloned.1.call-update) | async-done | bytes 2097168 | tf_op jit(solution)/shard_map/psum | solution.py:149
  162.9 17.0 %fusion.84 = f32[1024,512]{1,0:T(8,128)} fusion(f32[1024,1024]{1,0:T(8,128)} %copy-done.1, f32[1024,512]{0,1:T(8,128)} %all-reduce.5.cloned.1.call-done), kind=kOutput, calls=%fused_computation.120 | convolution fusion | flops 6442450944 | bytes 8388608 | tf_op jit(solution)/shard_map/dot_general | solution.py:39
  179.9 0.0 copy-done.2
  179.9 4.5 %fusion.83 = f32[512,512]{1,0:T(8,128)} fusion(f32[1024,512]{0,1:T(8,128)S(1)} %copy-done.2), kind=kOutput, calls=%fused_computation.119 | convolution fusion | flops 3221225472 | bytes 3145728 | tf_op jit(solution)/shard_map/dot_general | solution.py:39
  184.4 0.0 all-reduce.9.cloned.1.call-update
  184.5 87.5 %all-reduce.9.cloned.1.call-done = (f32[512,512]{1,0:T(8,128)}, f32[1024,512]{1,0:T(8,128)}) async-done(((f32[512,512]{1,0:T(8,128)}, f32[1024,512]{1,0:T(8,128)}), (f32[512,512]{1,0:T(8,128)}, f32[1024,512]{1,0:T(8,128)})) %all-reduce.9.cloned.1.call-update) | async-done | bytes 3145744 | tf_op jit(solution)/shard_map/psum | solution.py:152
  272.0 0.0 copy-start.3
  272.0 0.0 copy-start.6
  272.0 0.0 copy-start
  272.0 5.9 %fusion.85.normal_ref = f32[512,512]{1,0:T(8,128)S(1)} fusion(f32[1024,512]{1,0:T(8,128)} %get-tuple-element.11), kind=kOutput, calls=%fused_computation.121 | convolution fusion | flops 3221225472 | bytes 3145728 | tf_op jit(solution)/shard_map/dot_general | solution.py:39
  277.9 0.0 copy-done.3
  277.9 0.0 copy-done.6
  277.9 0.0 copy-start.5
  277.9 3.5 fusion.86.rhs_ref
  281.4 0.0 copy-done
  281.4 67.4 %factor_and_solve.1 = (f32[512,512]{1,0:T(8,128)}, f32[512,512]{1,0:T(8,128)S(1)}) custom-call(f32[512,512]{1,0:T(8,128)S(1)} %copy-done, f32[512,512]{1,0:T(8,128)S(1)} %fusion.85.normal_ref, f32[512,512]{1,0:T(8,128)S(1)} %fusion.86.rhs_ref), custom_call_target="tpu_custom_call" | custom-call | tf_op jit(solution)/shard_map/factor_and_solve/pallas_call | solution.py:105
  348.8 0.0 copy-done.5
  348.8 4.8 %convolution_subtract_fusion = f32[1024,512]{1,0:T(8,128)} fusion(f32[1024,512]{1,0:T(8,128)S(1)} %copy-done.5, f32[1024,512]{0,1:T(8,128)S(1)} %copy-done.2, f32[512,512]{1,0:T(8,128)S(1)} %get-tuple-element.8), kind=kOutput, calls=%fused_computation.40 | convolution fusion | flops 3221749760 | bytes 7340032 | tf_op jit(solution)/shard_map/dot_general | solution.py:156
Async XLA Ops:
  7.2 83.3 %all-reduce.5.cloned.1.call-start = ((), (), s32[]{:S(2)}) async-start(), calls=%async_computation | async-start | bytes 4194304 | tf_op jit(solution)/shard_map/psum | solution.py:148
  22.7 11.7 %copy-start.4 = (f32[1024,512]{1,0:T(8,128)S(1)}, f32[1024,512]{1,0:T(8,128)}, u32[]{:S(2)}) copy-start(f32[1024,512]{1,0:T(8,128)} %param.3) | copy-start | bytes 6291460
  22.8 140.2 %all-reduce.7.cloned.1.call-start = ((), (), s32[]{:S(2)}) async-start(), calls=%async_computation.1 | async-start | bytes 4194304 | tf_op jit(solution)/shard_map/psum | solution.py:149
  32.4 1.9 copy-start.1
  42.8 229.2 %all-reduce.9.cloned.1.call-start = ((), (), s32[]{:S(2)}) async-start(), calls=%async_computation.2 | async-start | bytes 6291456 | tf_op jit(solution)/shard_map/psum | solution.py:152
  90.5 89.4 %copy-start.2 = (f32[1024,512]{0,1:T(8,128)S(1)}, f32[1024,512]{0,1:T(8,128)}, u32[]{:S(2)}) copy-start(f32[1024,512]{0,1:T(8,128)} %all-reduce.5.cloned.1.call-done) | copy-start | bytes 6291460
  272.0 5.9 %copy-start.3 = (f32[1024,512]{1,0:T(8,128)S(1)}, f32[1024,512]{1,0:T(8,128)}, u32[]{:S(2)}) copy-start(f32[1024,512]{1,0:T(8,128)} %get-tuple-element.11) | copy-start | bytes 6291460
  272.0 5.9 %copy-start.6 = (f32[1024,512]{1,0:T(8,128)S(1)}, f32[1024,512]{1,0:T(8,128)}, u32[]{:S(2)}) copy-start(f32[1024,512]{1,0:T(8,128)} %all-reduce.7.cloned.1.call-done) | copy-start | bytes 6291460
  272.0 9.4 %copy-start = (f32[512,512]{1,0:T(8,128)S(1)}, f32[512,512]{1,0:T(8,128)}, u32[]{:S(2)}) copy-start(f32[512,512]{1,0:T(8,128)} %get-tuple-element.10.gram_ref) | copy-start | bytes 3145732
  277.9 71.0 %copy-start.5 = (f32[1024,512]{1,0:T(8,128)S(1)}, f32[1024,512]{1,0:T(8,128)}, u32[]{:S(2)}) copy-start(f32[1024,512]{1,0:T(8,128)} %param.3) | copy-start | bytes 6291460
Sparse Core Ops, SparseCore 0:
  22.9 67.5 all-reduce.4
  93.6 69.2 all-reduce.6
  184.6 87.3 all-reduce.8
